TPU v7x, 32 devices: a whole 2x2x4 slice. The times are simulated.
32 devices in a mesh: heads: 2 (over core), tm: 16 (over z, y, x).
Axes of the slice: x: 2, y: 2, z: 4, core: 2. Of those that a mesh axis runs over, the one named last changes fastest.
Arguments:
- queries: bfloat16 [4096, 768], P('tm', 'heads'), parts along dimension 1, may hold values from -8 to 8
- keys: bfloat16 [4096, 768], P('tm', 'heads'), parts along dimension 1, may hold values from -8 to 8
- values: bfloat16 [4096, 768], P('tm', 'heads'), parts along dimension 1, may hold values from -6 to 6
- positions: int32 [3, 4096], P(None, 'tm'), may hold values from 0 to 79, as said below
- tile_masks: int32 [32, 8, 2], P('tm'), may hold values from 0 to 1, as said below
- sink_index: int32 [256], replicated, may hold values from 0 to 3599, as said below
Outputs:
- attended: bfloat16 [4096, 768], P('tm', 'heads'), parts along dimension 1
There are 2 independent parts, one for each index of `heads`. A program takes and returns all parts, laid end to end along the dimension named above; an argument that names none is the same for every part. Nothing has to cross between parts.
Inputs may be any that keep to these rules, and one draw needn't show every extreme that they name: `positions`: consecutive tokens of the latent video of 33 x 45 x 80, row by row, from some starting token. `tile_masks`: tiles of farther partners are kept less often. `sink_index`: distinct rows among the first min(4096, 3600) of the window.
All inputs are finite; a program needn't handle non-finite values.
Results may differ from a plain program's by a relative error of at most 0.0085.
The roundings to bfloat16 on the way count: a program that leaves them out, or rounds other values in their place, can miss the bound.
Values may be sent and summed in bfloat16 or wider, within the bound.
No kernel may reach another device: no remote copies, remote signals or barrier semaphores. Data moves between devices by JAX's collectives and lax.ppermute only.
A program may use at most 64 MiB of HBM per device.

v0:
```python
import jax
import jax.numpy as jnp
from jax import lax
from jax.sharding import PartitionSpec as P

HG = 3
HD = 128
TILE = 128
NOFF = 4
SINK = 256


def shifted(shard, axis, by):
    length = lax.axis_size(axis)
    pairs = [(i, i + by) for i in range(length) if 0 <= i + by < length]
    return lax.ppermute(shard, axis, pairs)


def rotate(row_data, position, factor):
    row_count = row_data.shape[0]
    first_size = HD // 8
    second_size = (HD - HD // 8) // 2
    section_sizes = (first_size, second_size, HD - first_size - second_size)
    angle_list = []
    for axis_id in range(3):
        section_width = section_sizes[axis_id]
        inverse = 256.0 ** (-jnp.arange(0, section_width, 2).astype(jnp.float32) / section_width)
        angle_list.append(position[axis_id].astype(jnp.float32)[:, None] * inverse[None, :])
    angle_all = jnp.concatenate(angle_list, axis=1)
    cosine = jnp.cos(angle_all)[:, None, :]
    sine_part = jnp.sin(angle_all)[:, None, :]
    pair_view = row_data.astype(jnp.float32).reshape(row_count, HG, HD // 2, 2)
    even_part = pair_view[..., 0]
    odd_part = pair_view[..., 1]
    turned = jnp.stack(
        [even_part * cosine - odd_part * sine_part, even_part * sine_part + odd_part * cosine],
        axis=-1,
    )
    return (turned * factor).reshape(row_count, HG * HD)


def block_part(query_heads, key_heads, value_heads, tile_keep):
    keep_mask = jnp.repeat(jnp.repeat(tile_keep, TILE, axis=0), TILE, axis=1)[:, None, :]
    scores = jnp.einsum("qhd,khd->qhk", query_heads, key_heads, preferred_element_type=jnp.float32)
    masked = jnp.where(keep_mask > 0, scores, -1e30)
    row_max = jnp.max(masked, axis=2)
    weights = jnp.exp(masked - row_max[:, :, None]) * keep_mask
    totals = jnp.sum(weights, axis=2)
    weighted = jnp.einsum(
        "qhk,khd->qhd",
        weights.astype(jnp.bfloat16),
        value_heads,
        preferred_element_type=jnp.float32,
    )
    return (weighted, row_max, totals)


def combine_parts(first, second):
    weighted_a, max_a, total_a = first
    weighted_b, max_b, total_b = second
    new_max = jnp.maximum(max_a, max_b)
    scale_first = jnp.exp(max_a - new_max)
    scale_second = jnp.exp(max_b - new_max)
    weighted = weighted_a * scale_first[:, :, None] + weighted_b * scale_second[:, :, None]
    return (weighted, new_max, total_a * scale_first + total_b * scale_second)


def on_device(queries, keys, values, positions, tile_masks, sink_index):
    rows_here = queries.shape[0]
    shards = lax.axis_size("tm")
    index_here = lax.axis_index("tm")
    feature_width = HG * HD
    tiles = rows_here // TILE
    q_rot = rotate(queries, positions, HD ** (-0.5)).astype(jnp.bfloat16)
    k_rot = rotate(keys, positions, 1.0).astype(jnp.bfloat16)
    query_heads = q_rot.reshape(rows_here, HG, HD)
    key_heads = k_rot.reshape(rows_here, HG, HD)
    value_heads = values.reshape(rows_here, HG, HD)
    state = block_part(query_heads, key_heads, value_heads, jnp.ones((tiles, tiles), jnp.float32))
    local_index = sink_index - index_here * rows_here
    one_hot = (local_index[:, None] == jnp.arange(rows_here, dtype=jnp.int32)[None, :]).astype(
        jnp.bfloat16
    )
    sink_table = jnp.dot(
        one_hot, jnp.concatenate([k_rot, values], axis=1), preferred_element_type=jnp.float32
    )
    sink_table = lax.psum(sink_table, "tm").astype(jnp.bfloat16)
    sink_keys = sink_table[:, :feature_width].reshape(SINK, HG, HD)
    sink_values = sink_table[:, feature_width:].reshape(SINK, HG, HD)
    sink_keep = jnp.ones((tiles, SINK // TILE), jnp.float32)
    state = combine_parts(state, block_part(query_heads, sink_keys, sink_values, sink_keep))
    mask_float = tile_masks.astype(jnp.float32)
    for offset in range(1, NOFF + 1):
        later_rows, later_values = shifted((k_rot, values), "tm", -offset)
        earlier_rows, earlier_values = shifted((k_rot, values), "tm", offset)
        later_ok = (index_here + offset < shards).astype(jnp.float32)
        earlier_ok = (index_here - offset >= 0).astype(jnp.float32)
        later_part = block_part(
            query_heads,
            later_rows.reshape(rows_here, HG, HD),
            later_values.reshape(rows_here, HG, HD),
            mask_float[:, offset - 1, :] * later_ok,
        )
        state = combine_parts(state, later_part)
        earlier_part = block_part(
            query_heads,
            earlier_rows.reshape(rows_here, HG, HD),
            earlier_values.reshape(rows_here, HG, HD),
            mask_float[:, NOFF + offset - 1, :] * earlier_ok,
        )
        state = combine_parts(state, earlier_part)
    weighted, row_max, totals = state
    return (weighted / totals[:, :, None]).astype(jnp.bfloat16).reshape(rows_here, feature_width)


def solution(mesh):
    in_specs = (
        P("tm", "heads"),
        P("tm", "heads"),
        P("tm", "heads"),
        P(None, "tm"),
        P("tm", None, None),
        P(),
    )
    out_specs = P("tm", "heads")
    return jax.shard_map(
        on_device, mesh=mesh, in_specs=in_specs, out_specs=out_specs, check_vma=False
    )
```

profile of v0, /device:TPU:0, one launch (start us, length us, event | category | flops | bytes accessed | tf_op | source)
XLA Modules:
  0.0 197.0 jit_solution(17712258259752564068)
XLA Ops:
  3.6 5.8 %collective-permute-start.10 = (bf16[256,384]{0,1:T(8,128)(2,1)S(1)}, bf16[256,384]{0,1:T(8,128)(2,1)S(1)}, u32[]{:S(2)}, u32[]{:S(2)}) collective-permute-start(bf16[256,384]{0,1:T(8,128)(2,1)S(1)} %convert_element_type.149), channel_id=1, source_target_pairs={{0,3},{1,4},{2,5},{3,6},{4,7},{5,8},{6,9},{7,10},{8,11},{9,12},{10... | collective-permute-start | bytes 589832 | tf_op jit(solution)/shard_map/ppermute | solution.py:16
  9.4 1.3 collective-permute-start.8
  10.7 4.1 %collective-permute-start.6 = (bf16[256,384]{0,1:T(8,128)(2,1)S(1)}, bf16[256,384]{0,1:T(8,128)(2,1)}, u32[]{:S(2)}, u32[]{:S(2)}) collective-permute-start(bf16[256,384]{0,1:T(8,128)(2,1)S(1)} %convert_element_type.149), channel_id=1, source_target_pairs={{0,2},{1,3},{2,4},{3,5},{4,6},{5,7},{6,8},{7,9},{8,10},{9,11},{10,... | collective-permute-start | bytes 589832 | tf_op jit(solution)/shard_map/ppermute | solution.py:16
  14.8 1.3 collective-permute-start.4
  16.1 5.2 %collective-permute-start.2 = (bf16[256,384]{0,1:T(8,128)(2,1)S(1)}, bf16[256,384]{0,1:T(8,128)(2,1)}, u32[]{:S(2)}, u32[]{:S(2)}) collective-permute-start(bf16[256,384]{0,1:T(8,128)(2,1)S(1)} %convert_element_type.149), channel_id=1, source_target_pairs={{0,1},{1,2},{2,3},{3,4},{4,5},{5,6},{6,7},{7,8},{8,9},{9,10},{10,1... | collective-permute-start | bytes 589832 | tf_op jit(solution)/shard_map/ppermute | solution.py:16
  26.4 85.1 %all-reduce.1 = bf16[256,768]{1,0:T(8,128)(2,1)S(1)} all-reduce(f32[256,768]{1,0:T(8,128)S(1)} %fusion.68), channel_id=1, replica_groups=mesh['heads'=2,'tm'=16] {'tm'}, use_global_device_ids=true, to_apply=%region_1.2 | all-reduce | flops 196608 | bytes 1179648 | tf_op jit(solution)/shard_map/psum | solution.py:87
  118.9 1.3 collective-permute-start
  120.5 1.3 collective-permute-start.12
  121.9 1.3 fusion.102
  123.2 4.6 %collective-permute-start.14 = (bf16[256,384]{0,1:T(8,128)(2,1)S(1)}, bf16[256,384]{0,1:T(8,128)(2,1)S(1)}, u32[]{:S(2)}, u32[]{:S(2)}) collective-permute-start(bf16[256,384]{0,1:T(8,128)(2,1)S(1)} %convert_element_type.149), channel_id=1, source_target_pairs={{0,4},{1,5},{2,6},{3,7},{4,8},{5,9},{6,10},{7,11},{8,12},{9,13},{1... | collective-permute-start | bytes 589832 | tf_op jit(solution)/shard_map/ppermute | solution.py:16
  127.7 1.3 fusion.103
  129.1 4.5 %collective-permute-start.3 = (bf16[256,384]{1,0:T(8,128)(2,1)}, bf16[256,384]{1,0:T(8,128)(2,1)S(1)}, u32[]{:S(2)}, u32[]{:S(2)}) collective-permute-start(bf16[256,384]{1,0:T(8,128)(2,1)} %param.8), channel_id=1, source_target_pairs={{0,1},{1,2},{2,3},{3,4},{4,5},{5,6},{6,7},{7,8},{8,9},{9,10},{10,1... | collective-permute-start | bytes 589832 | tf_op jit(solution)/shard_map/ppermute | solution.py:16
  133.6 1.3 fusion.104
  135.0 1.3 collective-permute-start.5
  136.3 1.3 fusion.105
  137.6 5.2 %collective-permute-start.7 = (bf16[256,384]{1,0:T(8,128)(2,1)}, bf16[256,384]{1,0:T(8,128)(2,1)}, u32[]{:S(2)}, u32[]{:S(2)}) collective-permute-start(bf16[256,384]{1,0:T(8,128)(2,1)} %param.8), channel_id=1, source_target_pairs={{0,2},{1,3},{2,4},{3,5},{4,6},{5,7},{6,8},{7,9},{8,10},{9,11},{10,... | collective-permute-start | bytes 589832 | tf_op jit(solution)/shard_map/ppermute | solution.py:16
  143.2 1.3 collective-permute-start.9
  144.9 6.1 %collective-permute-start.11 = (bf16[256,384]{1,0:T(8,128)(2,1)}, bf16[256,384]{1,0:T(8,128)(2,1)}, u32[]{:S(2)}, u32[]{:S(2)}) collective-permute-start(bf16[256,384]{1,0:T(8,128)(2,1)} %param.8), channel_id=1, source_target_pairs={{0,3},{1,4},{2,5},{3,6},{4,7},{5,8},{6,9},{7,10},{8,11},{9,12},{10... | collective-permute-start | bytes 589832 | tf_op jit(solution)/shard_map/ppermute | solution.py:16
  163.2 1.3 collective-permute-start.13
  165.6 2.2 %fusion.11 = f32[256,3,128]{0,2,1:T(8,128)} fusion(bf16[256,3,128]{0,2,1:T(8,128)(2,1)S(1)} %bitcast.276, f32[256,3,256]{0,2,1:T(8,128)} %copy-done.7, f32[256,256]{0,1:T(8,128)S(1)} %bitcast.272, f32[256,3]{0,1:T(4,128)S(1)} %copy-done.46, f32[256,3]{0,1:T(4,128)S(1)} %get-tuple-element.17), kind=kOutput, calls=%fused_computation.31 | convolution fusion | flops 51019776 | bytes 1644544 | tf_op jit(solution)/shard_map/qhk,khd->qhd/dot_general | solution.py:49
  167.8 5.2 %collective-permute-start.15 = (bf16[256,384]{1,0:T(8,128)(2,1)}, bf16[256,384]{1,0:T(8,128)(2,1)}, u32[]{:S(2)}, u32[]{:S(2)}) collective-permute-start(bf16[256,384]{1,0:T(8,128)(2,1)} %param.8), channel_id=1, source_target_pairs={{0,4},{1,5},{2,6},{3,7},{4,8},{5,9},{6,10},{7,11},{8,12},{9,13},{1... | collective-permute-start | bytes 589832 | tf_op jit(solution)/shard_map/ppermute | solution.py:16
  173.0 1.7 copy.67
  174.8 2.4 %fusion.12 = f32[256,3,128]{0,2,1:T(8,128)} fusion(bf16[256,3,128]{0,2,1:T(8,128)(2,1)} %bitcast.277, f32[256,3,256]{0,2,1:T(8,128)} %copy-done.6, f32[256,256]{0,1:T(8,128)} %bitcast.270, f32[256,3]{0,1:T(4,128)S(1)} %copy-done.44, f32[256,3]{0,1:T(4,128)S(1)} %get-tuple-element.18), kind=kOutput, calls=%fused_computation.32 | convolution fusion | flops 51019776 | bytes 1644544 | tf_op jit(solution)/shard_map/qhk,khd->qhd/dot_general | solution.py:49
  177.1 1.3 collective-permute-start.1
  178.4 1.7 copy.72
  180.2 2.1 %fusion.13 = f32[256,3,128]{0,2,1:T(8,128)} fusion(bf16[256,3,128]{0,2,1:T(8,128)(2,1)} %bitcast.278, f32[256,3,256]{0,2,1:T(8,128)S(1)} %copy-done.1, f32[256,256]{0,1:T(8,128)} %bitcast.268, f32[256,3]{0,1:T(4,128)S(1)} %copy-done.42, f32[256,3]{0,1:T(4,128)S(1)} %get-tuple-element.19), kind=kOutput, calls=%fused_computation.33 | convolution fusion | flops 51019776 | bytes 1644544 | tf_op jit(solution)/shard_map/qhk,khd->qhd/dot_general | solution.py:49
  182.3 1.1 copy.77
  184.4 1.1 copy.82
  188.8 1.8 copy.92
  190.6 2.0 %fusion.17 = f32[256,3,128]{0,2,1:T(8,128)} fusion(bf16[256,3,128]{0,2,1:T(8,128)(2,1)} %bitcast.282, f32[256,3,256]{0,2,1:T(8,128)S(1)} %copy-done.5, f32[256,256]{0,1:T(8,128)S(1)} %bitcast.260, f32[256,3]{0,1:T(4,128)S(1)} %get-tuple-element.49, f32[256,3]{0,1:T(4,128)S(1)} %get-tuple-element.23), kind=kOutput, calls=%fused_computation.37 | convolution fusion | flops 51019776 | bytes 1644544 | tf_op jit(solution)/shard_map/qhk,khd->qhd/dot_general | solution.py:49
  192.6 1.1 copy.57
  194.4 1.8 fusion.36
  (236 shorter events, 35.7 us)
Async XLA Ops:
  3.6 115.3 %collective-permute-start.10 = (bf16[256,384]{0,1:T(8,128)(2,1)S(1)}, bf16[256,384]{0,1:T(8,128)(2,1)S(1)}, u32[]{:S(2)}, u32[]{:S(2)}) collective-permute-start(bf16[256,384]{0,1:T(8,128)(2,1)S(1)} %convert_element_type.149), channel_id=1, source_target_pairs={{0,3},{1,4},{2,5},{3,6},{4,7},{5,8},{6,9},{7,10},{8,11},{9,12},{10... | collective-permute-start | bytes 589832 | tf_op jit(solution)/shard_map/ppermute | solution.py:16
  9.4 111.1 %collective-permute-start.8 = (bf16[256,384]{0,1:T(8,128)(2,1)S(1)}, bf16[256,384]{0,1:T(8,128)(2,1)S(1)}, u32[]{:S(2)}, u32[]{:S(2)}) collective-permute-start(bf16[256,384]{0,1:T(8,128)(2,1)S(1)} %convert_element_type.149), channel_id=1, source_target_pairs={{3,0},{4,1},{5,2},{6,3},{7,4},{8,5},{9,6},{10,7},{11,8},{12,9},{13... | collective-permute-start | bytes 589832 | tf_op jit(solution)/shard_map/ppermute | solution.py:16
  10.7 112.4 %collective-permute-start.6 = (bf16[256,384]{0,1:T(8,128)(2,1)S(1)}, bf16[256,384]{0,1:T(8,128)(2,1)}, u32[]{:S(2)}, u32[]{:S(2)}) collective-permute-start(bf16[256,384]{0,1:T(8,128)(2,1)S(1)} %convert_element_type.149), channel_id=1, source_target_pairs={{0,2},{1,3},{2,4},{3,5},{4,6},{5,7},{6,8},{7,9},{8,10},{9,11},{10,... | collective-permute-start | bytes 589832 | tf_op jit(solution)/shard_map/ppermute | solution.py:16
  14.8 114.2 %collective-permute-start.4 = (bf16[256,384]{0,1:T(8,128)(2,1)S(1)}, bf16[256,384]{0,1:T(8,128)(2,1)}, u32[]{:S(2)}, u32[]{:S(2)}) collective-permute-start(bf16[256,384]{0,1:T(8,128)(2,1)S(1)} %convert_element_type.149), channel_id=1, source_target_pairs={{2,0},{3,1},{4,2},{5,3},{6,4},{7,5},{8,6},{9,7},{10,8},{11,9},{12,... | collective-permute-start | bytes 589832 | tf_op jit(solution)/shard_map/ppermute | solution.py:16
  16.1 118.8 %collective-permute-start.2 = (bf16[256,384]{0,1:T(8,128)(2,1)S(1)}, bf16[256,384]{0,1:T(8,128)(2,1)}, u32[]{:S(2)}, u32[]{:S(2)}) collective-permute-start(bf16[256,384]{0,1:T(8,128)(2,1)S(1)} %convert_element_type.149), channel_id=1, source_target_pairs={{0,1},{1,2},{2,3},{3,4},{4,5},{5,6},{6,7},{7,8},{8,9},{9,10},{10,1... | collective-permute-start | bytes 589832 | tf_op jit(solution)/shard_map/ppermute | solution.py:16
  112.0 6.7 %copy-start.8 = (f32[256,3,256]{0,2,1:T(8,128)}, f32[256,3,256]{0,2,1:T(8,128)S(1)}, u32[]{:S(2)}) copy-start(f32[256,3,256]{0,2,1:T(8,128)S(1)} %get-tuple-element.66) | copy-start | bytes 2359300
  118.9 18.7 %collective-permute-start = (bf16[256,384]{0,1:T(8,128)(2,1)S(1)}, bf16[256,384]{0,1:T(8,128)(2,1)S(1)}, u32[]{:S(2)}, u32[]{:S(2)}) collective-permute-start(bf16[256,384]{0,1:T(8,128)(2,1)S(1)} %convert_element_type.149), channel_id=1, source_target_pairs={{1,0},{2,1},{3,2},{4,3},{5,4},{6,5},{7,6},{8,7},{9,8},{10,9},{11,1... | collective-permute-start | bytes 589832 | tf_op jit(solution)/shard_map/ppermute | solution.py:16
  120.5 22.6 %collective-permute-start.12 = (bf16[256,384]{0,1:T(8,128)(2,1)S(1)}, bf16[256,384]{0,1:T(8,128)(2,1)S(1)}, u32[]{:S(2)}, u32[]{:S(2)}) collective-permute-start(bf16[256,384]{0,1:T(8,128)(2,1)S(1)} %convert_element_type.149), channel_id=1, source_target_pairs={{4,0},{5,1},{6,2},{7,3},{8,4},{9,5},{10,6},{11,7},{12,8},{13,9},{1... | collective-permute-start | bytes 589832 | tf_op jit(solution)/shard_map/ppermute | solution.py:16
  121.8 5.9 %copy-start.34 = (pred[256,256]{0,1:T(8,128)(4,1)S(1)}, pred[256,256]{0,1:T(8,128)(4,1)}, u32[]{:S(2)}) copy-start(pred[256,256]{0,1:T(8,128)(4,1)} %bitcast_compare_fusion.4) | copy-start | bytes 196612
  123.2 21.7 %collective-permute-start.14 = (bf16[256,384]{0,1:T(8,128)(2,1)S(1)}, bf16[256,384]{0,1:T(8,128)(2,1)S(1)}, u32[]{:S(2)}, u32[]{:S(2)}) collective-permute-start(bf16[256,384]{0,1:T(8,128)(2,1)S(1)} %convert_element_type.149), channel_id=1, source_target_pairs={{0,4},{1,5},{2,6},{3,7},{4,8},{5,9},{6,10},{7,11},{8,12},{9,13},{1... | collective-permute-start | bytes 589832 | tf_op jit(solution)/shard_map/ppermute | solution.py:16
  127.7 5.9 %copy-start.33 = (pred[256,256]{0,1:T(8,128)(4,1)S(1)}, pred[256,256]{0,1:T(8,128)(4,1)}, u32[]{:S(2)}) copy-start(pred[256,256]{0,1:T(8,128)(4,1)} %bitcast_compare_fusion.5) | copy-start | bytes 196612
  129.0 25.8 %copy-start = (f32[256,3,256]{0,2,1:T(8,128)}, f32[256,3,256]{0,2,1:T(8,128)S(1)}, u32[]{:S(2)}) copy-start(f32[256,3,256]{0,2,1:T(8,128)S(1)} %get-tuple-element.58) | copy-start | bytes 2359300
  129.0 30.6 %copy-start.41 = (f32[256,3]{0,1:T(4,128)}, f32[256,3]{0,1:T(4,128)S(1)}, u32[]{:S(2)}) copy-start(f32[256,3]{0,1:T(4,128)S(1)} %get-tuple-element.57) | copy-start | bytes 9220
  129.1 33.5 %collective-permute-start.3 = (bf16[256,384]{1,0:T(8,128)(2,1)}, bf16[256,384]{1,0:T(8,128)(2,1)S(1)}, u32[]{:S(2)}, u32[]{:S(2)}) collective-permute-start(bf16[256,384]{1,0:T(8,128)(2,1)} %param.8), channel_id=1, source_target_pairs={{0,1},{1,2},{2,3},{3,4},{4,5},{5,6},{6,7},{7,8},{8,9},{9,10},{10,1... | collective-permute-start | bytes 589832 | tf_op jit(solution)/shard_map/ppermute | solution.py:16
  134.9 19.9 %copy-start.6 = (f32[256,3,256]{0,2,1:T(8,128)}, f32[256,3,256]{0,2,1:T(8,128)S(1)}, u32[]{:S(2)}) copy-start(f32[256,3,256]{0,2,1:T(8,128)S(1)} %get-tuple-element.60) | copy-start | bytes 2359300
  134.9 24.7 %copy-start.43 = (f32[256,3]{0,1:T(4,128)}, f32[256,3]{0,1:T(4,128)S(1)}, u32[]{:S(2)}) copy-start(f32[256,3]{0,1:T(4,128)S(1)} %get-tuple-element.59) | copy-start | bytes 9220
  135.0 32.9 %collective-permute-start.5 = (bf16[256,384]{1,0:T(8,128)(2,1)}, bf16[256,384]{1,0:T(8,128)(2,1)}, u32[]{:S(2)}, u32[]{:S(2)}) collective-permute-start(bf16[256,384]{1,0:T(8,128)(2,1)} %param.8), channel_id=1, source_target_pairs={{2,0},{3,1},{4,2},{5,3},{6,4},{7,5},{8,6},{9,7},{10,8},{11,9},{12,... | collective-permute-start | bytes 589832 | tf_op jit(solution)/shard_map/ppermute | solution.py:16
  136.3 6.6 %copy-start.31 = (pred[256,256]{0,1:T(8,128)(4,1)S(1)}, pred[256,256]{0,1:T(8,128)(4,1)}, u32[]{:S(2)}) copy-start(pred[256,256]{0,1:T(8,128)(4,1)} %bitcast_compare_fusion.7) | copy-start | bytes 196612
  137.6 15.2 %copy-start.7 = (f32[256,3,256]{0,2,1:T(8,128)}, f32[256,3,256]{0,2,1:T(8,128)S(1)}, u32[]{:S(2)}) copy-start(f32[256,3,256]{0,2,1:T(8,128)S(1)} %get-tuple-element.62) | copy-start | bytes 2359300
  137.6 22.1 %copy-start.45 = (f32[256,3]{0,1:T(4,128)}, f32[256,3]{0,1:T(4,128)S(1)}, u32[]{:S(2)}) copy-start(f32[256,3]{0,1:T(4,128)S(1)} %get-tuple-element.61) | copy-start | bytes 9220
  137.6 39.6 %collective-permute-start.7 = (bf16[256,384]{1,0:T(8,128)(2,1)}, bf16[256,384]{1,0:T(8,128)(2,1)}, u32[]{:S(2)}, u32[]{:S(2)}) collective-permute-start(bf16[256,384]{1,0:T(8,128)(2,1)} %param.8), channel_id=1, source_target_pairs={{0,2},{1,3},{2,4},{3,5},{4,6},{5,7},{6,8},{7,9},{8,10},{9,11},{10,... | collective-permute-start | bytes 589832 | tf_op jit(solution)/shard_map/ppermute | solution.py:16
  143.2 16.5 %copy-start.39 = (f32[256,3]{0,1:T(4,128)}, f32[256,3]{0,1:T(4,128)S(1)}, u32[]{:S(2)}) copy-start(f32[256,3]{0,1:T(4,128)S(1)} %get-tuple-element.63) | copy-start | bytes 9220
  143.2 39.1 %collective-permute-start.9 = (bf16[256,384]{1,0:T(8,128)(2,1)}, bf16[256,384]{1,0:T(8,128)(2,1)}, u32[]{:S(2)}, u32[]{:S(2)}) collective-permute-start(bf16[256,384]{1,0:T(8,128)(2,1)} %param.8), channel_id=1, source_target_pairs={{3,0},{4,1},{5,2},{6,3},{7,4},{8,5},{9,6},{10,7},{11,8},{12,9},{13... | collective-permute-start | bytes 589832 | tf_op jit(solution)/shard_map/ppermute | solution.py:16
  144.5 6.5 %copy-start.29 = (pred[256,256]{0,1:T(8,128)(4,1)S(1)}, pred[256,256]{0,1:T(8,128)(4,1)}, u32[]{:S(2)}) copy-start(pred[256,256]{0,1:T(8,128)(4,1)} %bitcast_compare_fusion) | copy-start | bytes 196612
  144.8 14.1 %copy-start.2 = (f32[256,3,256]{0,2,1:T(8,128)}, f32[256,3,256]{0,2,1:T(8,128)S(1)}, u32[]{:S(2)}) copy-start(f32[256,3,256]{0,2,1:T(8,128)S(1)} %get-tuple-element.52) | copy-start | bytes 2359300
  144.8 14.8 %copy-start.47 = (f32[256,3]{0,1:T(4,128)}, f32[256,3]{0,1:T(4,128)S(1)}, u32[]{:S(2)}) copy-start(f32[256,3]{0,1:T(4,128)S(1)} %get-tuple-element.51) | copy-start | bytes 9220
  144.9 39.6 %collective-permute-start.11 = (bf16[256,384]{1,0:T(8,128)(2,1)}, bf16[256,384]{1,0:T(8,128)(2,1)}, u32[]{:S(2)}, u32[]{:S(2)}) collective-permute-start(bf16[256,384]{1,0:T(8,128)(2,1)} %param.8), channel_id=1, source_target_pairs={{0,3},{1,4},{2,5},{3,6},{4,7},{5,8},{6,9},{7,10},{8,11},{9,12},{10... | collective-permute-start | bytes 589832 | tf_op jit(solution)/shard_map/ppermute | solution.py:16
  151.3 7.6 %copy-start.4 = (f32[256,3,256]{0,2,1:T(8,128)}, f32[256,3,256]{0,2,1:T(8,128)S(1)}, u32[]{:S(2)}) copy-start(f32[256,3,256]{0,2,1:T(8,128)S(1)} %get-tuple-element.50) | copy-start | bytes 2359300
  163.2 23.3 %collective-permute-start.13 = (bf16[256,384]{1,0:T(8,128)(2,1)}, bf16[256,384]{1,0:T(8,128)(2,1)}, u32[]{:S(2)}, u32[]{:S(2)}) collective-permute-start(bf16[256,384]{1,0:T(8,128)(2,1)} %param.8), channel_id=1, source_target_pairs={{4,0},{5,1},{6,2},{7,3},{8,4},{9,5},{10,6},{11,7},{12,8},{13,9},{1... | collective-permute-start | bytes 589832 | tf_op jit(solution)/shard_map/ppermute | solution.py:16
  167.8 20.9 %collective-permute-start.15 = (bf16[256,384]{1,0:T(8,128)(2,1)}, bf16[256,384]{1,0:T(8,128)(2,1)}, u32[]{:S(2)}, u32[]{:S(2)}) collective-permute-start(bf16[256,384]{1,0:T(8,128)(2,1)} %param.8), channel_id=1, source_target_pairs={{0,4},{1,5},{2,6},{3,7},{4,8},{5,9},{6,10},{7,11},{8,12},{9,13},{1... | collective-permute-start | bytes 589832 | tf_op jit(solution)/shard_map/ppermute | solution.py:16
  174.8 5.4 %copy-start.1 = (f32[256,3,256]{0,2,1:T(8,128)S(1)}, f32[256,3,256]{0,2,1:T(8,128)}, u32[]{:S(2)}) copy-start(f32[256,3,256]{0,2,1:T(8,128)} %copy-done) | copy-start | bytes 2359300
  177.1 15.5 %collective-permute-start.1 = (bf16[256,384]{1,0:T(8,128)(2,1)}, bf16[256,384]{1,0:T(8,128)(2,1)}, u32[]{:S(2)}, u32[]{:S(2)}) collective-permute-start(bf16[256,384]{1,0:T(8,128)(2,1)} %param.8), channel_id=1, source_target_pairs={{1,0},{2,1},{3,2},{4,3},{5,4},{6,5},{7,6},{8,7},{9,8},{10,9},{11,1... | collective-permute-start | bytes 589832 | tf_op jit(solution)/shard_map/ppermute | solution.py:16
  (51 other events, 61.2 us)
where the time goes:
time: 198 us; the launch traced here: 197 us
  blocking collectives  85.1 us (43%)
  starting transfers between devices  51.1 us (26%)
  local copies, waits for them, and re-layouts  28.5 us (14%)
  matrix products  22.2 us (11%)
  other arithmetic  9.08 us (5%)
    psum x1, blocking collectives, on_device(): sink_table = lax.psum(sink_table, 'tm').astype(jnp.bfloat16)  85.1 us
    ppermute x16, starting transfers between devices, shifted(): return lax.ppermute(shard, axis, pairs)  51.1 us
    dot_general x10, matrix products, block_part(): jnp.einsum('qhk,khd->qhd', weights.astype(jnp.bfloat16), value_heads, pre...  14.8 us
    unnamed x151, local copies, waits for them, and re-layouts  13.1 us
    ppermute x8, local copies, waits for them, and re-layouts, shifted(): return lax.ppermute(shard, axis, pairs)  10.8 us
    dot_general x10, matrix products, block_part(): jnp.einsum('qhd,khd->qhk', query_heads, key_heads, preferred_element_type...  7.07 us
    gt x8, other arithmetic, block_part(): masked = jnp.where(keep_mask > 0, scores, -1e+30)  4.55 us
  transfers between devices with their start and end apart: 16, of which 0 were waited for; matrix products, arithmetic and copies ran while one was open for 21% of the time, Pallas kernels for 0%

commit v1 on v0

--- a/solution.py
+++ b/solution.py
@@ -8,6 +8,10 @@
 TILE = 128
 NOFF = 4
 SINK = 256
+
+
+def weights_begin(local_x):
+    return lax.all_gather(local_x, "tm").sum(axis=0)
 
 
 def shifted(shard, axis, by):
@@ -84,7 +88,7 @@
     sink_table = jnp.dot(
         one_hot, jnp.concatenate([k_rot, values], axis=1), preferred_element_type=jnp.float32
     )
-    sink_table = lax.psum(sink_table, "tm").astype(jnp.bfloat16)
+    sink_table = weights_begin(sink_table).astype(jnp.bfloat16)
     sink_keys = sink_table[:, :feature_width].reshape(SINK, HG, HD)
     sink_values = sink_table[:, feature_width:].reshape(SINK, HG, HD)
     sink_keep = jnp.ones((tiles, SINK // TILE), jnp.float32)

time: 198 us -> 234 us (1.18)
  waiting for transfers between devices: 0.04 us -> 96.6 us
  blocking collectives: 85.1 us -> 0 us
  between operations: 0.98 us -> 14.3 us
  other arithmetic: 9.08 us -> 20 us
  local copies, waits for them, and re-layouts: 28.5 us -> 23.5 us
  starting transfers between devices: 51.1 us -> 55.2 us
    psum x1 -> x0, blocking collectives: 85.1 us -> none  [on_device(): sink_table = lax.psum(sink_table, 'tm').astype(jnp.bfloat16)]
    all_gather x0 -> x1, waiting for transfers between devices: none -> 81.9 us  [weights_begin(): return lax.all_gather(local_x, 'tm').sum(axis=0)]
    ppermute x16, waiting for transfers between devices: 0.04 us -> 14.7 us  [shifted(): return lax.ppermute(shard, axis, pairs)]
    unnamed x151 -> x95, local copies, waits for them, and re-layouts: 13.1 us -> 2.74 us
    reduce_sum x0 -> x1, other arithmetic: none -> 6.21 us  [weights_begin(): return lax.all_gather(local_x, 'tm').sum(axis=0)]
    ppermute x16, starting transfers between devices: 51.1 us -> 55.2 us  [shifted(): return lax.ppermute(shard, axis, pairs)]
    dot_general x10, matrix products: 14.8 us -> 11.1 us  [block_part(): jnp.einsum('qhk,khd->qhd', weights.astype(jnp.bfloat16), value_heads, pre...]
    reduce_sum x5, other arithmetic: 1.35 us -> 4.97 us  [block_part(): totals = jnp.sum(weights, axis=2)]
  transfers between devices with their start and end apart: 16 -> 17, of which waited for: 0 -> 4; matrix products, arithmetic and copies ran while one was open for 21% -> 12% of each run, Pallas kernels for 0% -> 0%
where the time goes in v1:
time: 234 us; the launch traced here: 232 us
  waiting for transfers between devices  96.6 us (41%)
  starting transfers between devices  55.2 us (24%)
  local copies, waits for them, and re-layouts  23.5 us (10%)
  matrix products  22.8 us (10%)
  other arithmetic  20 us (9%)
  between operations  14.3 us (6%)
    all_gather x1, waiting for transfers between devices, weights_begin(): return lax.all_gather(local_x, 'tm').sum(axis=0)  81.9 us
    ppermute x16, starting transfers between devices, shifted(): return lax.ppermute(shard, axis, pairs)  55.2 us
    ppermute x16, waiting for transfers between devices, shifted(): return lax.ppermute(shard, axis, pairs)  14.7 us
    dot_general x10, matrix products, block_part(): jnp.einsum('qhk,khd->qhd', weights.astype(jnp.bfloat16), value_heads, pre...  11.1 us
    dot_general x10, matrix products, block_part(): jnp.einsum('qhd,khd->qhk', query_heads, key_heads, preferred_element_type...  9.48 us
    ppermute x8, local copies, waits for them, and re-layouts, shifted(): return lax.ppermute(shard, axis, pairs)  7.47 us
    reduce_sum x1, other arithmetic, weights_begin(): return lax.all_gather(local_x, 'tm').sum(axis=0)  6.21 us
    reduce_sum x5, other arithmetic, block_part(): totals = jnp.sum(weights, axis=2)  4.97 us
  transfers between devices with their start and end apart: 17, of which 4 were waited for; matrix products, arithmetic and copies ran while one was open for 12% of the time, Pallas kernels for 0%

profile of v1, /device:TPU:0, one launch (start us, length us, event | category | flops | bytes accessed | tf_op | source)
XLA Modules:
  0.0 232.3 jit_solution(11326038386474494109)
XLA Ops:
  12.6 2.1 fusion.68
  14.7 5.8 %collective-permute-start.10 = (bf16[256,384]{0,1:T(8,128)(2,1)}, bf16[256,384]{0,1:T(8,128)(2,1)S(1)}, u32[]{:S(2)}, u32[]{:S(2)}) collective-permute-start(bf16[256,384]{0,1:T(8,128)(2,1)} %convert_element_type.149), channel_id=1, source_target_pairs={{0,3},{1,4},{2,5},{3,6},{4,7},{5,8},{6,9},{7,10},{8,11},{9,12},{10... | collective-permute-start | bytes 589832 | tf_op jit(solution)/shard_map/ppermute | solution.py:20
  20.6 2.5 %collective-permute-start.3 = (bf16[256,384]{1,0:T(8,128)(2,1)}, bf16[256,384]{1,0:T(8,128)(2,1)S(1)}, u32[]{:S(2)}, u32[]{:S(2)}) collective-permute-start(bf16[256,384]{1,0:T(8,128)(2,1)} %param.8), channel_id=1, source_target_pairs={{0,1},{1,2},{2,3},{3,4},{4,5},{5,6},{6,7},{7,8},{8,9},{9,10},{10,1... | collective-permute-start | bytes 589832 | tf_op jit(solution)/shard_map/ppermute | solution.py:20
  23.1 1.3 collective-permute-start.5
  24.4 4.6 %collective-permute-start.7 = (bf16[256,384]{1,0:T(8,128)(2,1)}, bf16[256,384]{1,0:T(8,128)(2,1)S(1)}, u32[]{:S(2)}, u32[]{:S(2)}) collective-permute-start(bf16[256,384]{1,0:T(8,128)(2,1)} %param.8), channel_id=1, source_target_pairs={{0,2},{1,3},{2,4},{3,5},{4,6},{5,7},{6,8},{7,9},{8,10},{9,11},{10,... | collective-permute-start | bytes 589832 | tf_op jit(solution)/shard_map/ppermute | solution.py:20
  37.5 7.4 %collective-permute-start.11 = (bf16[256,384]{1,0:T(8,128)(2,1)}, bf16[256,384]{1,0:T(8,128)(2,1)}, u32[]{:S(2)}, u32[]{:S(2)}) collective-permute-start(bf16[256,384]{1,0:T(8,128)(2,1)} %param.8), channel_id=1, source_target_pairs={{0,3},{1,4},{2,5},{3,6},{4,7},{5,8},{6,9},{7,10},{8,11},{9,12},{10... | collective-permute-start | bytes 589832 | tf_op jit(solution)/shard_map/ppermute | solution.py:20
  46.2 7.0 %collective-permute-start.15 = (bf16[256,384]{1,0:T(8,128)(2,1)}, bf16[256,384]{1,0:T(8,128)(2,1)S(1)}, u32[]{:S(2)}, u32[]{:S(2)}) collective-permute-start(bf16[256,384]{1,0:T(8,128)(2,1)} %param.8), channel_id=1, source_target_pairs={{0,4},{1,5},{2,6},{3,7},{4,8},{5,9},{6,10},{7,11},{8,12},{9,13},{1... | collective-permute-start | bytes 589832 | tf_op jit(solution)/shard_map/ppermute | solution.py:20
  53.4 1.3 collective-permute-start.1
  59.5 1.7 copy.131
  61.3 2.5 %collective-permute-done.13 = bf16[256,384]{1,0:T(8,128)(2,1)S(1)} collective-permute-done((bf16[256,384]{1,0:T(8,128)(2,1)}, bf16[256,384]{1,0:T(8,128)(2,1)S(1)}, u32[]{:S(2)}, u32[]{:S(2)}) %collective-permute-start.13) | collective-permute-done | bytes 196640 | tf_op jit(solution)/shard_map/ppermute | solution.py:20
  63.8 3.6 %collective-permute-start.6 = (bf16[256,384]{0,1:T(8,128)(2,1)}, bf16[256,384]{0,1:T(8,128)(2,1)S(1)}, u32[]{:S(2)}, u32[]{:S(2)}) collective-permute-start(bf16[256,384]{0,1:T(8,128)(2,1)} %convert_element_type.149), channel_id=1, source_target_pairs={{0,2},{1,3},{2,4},{3,5},{4,6},{5,7},{6,8},{7,9},{8,10},{9,11},{10,... | collective-permute-start | bytes 589832 | tf_op jit(solution)/shard_map/ppermute | solution.py:20
  70.4 5.2 %collective-permute-start.2 = (bf16[256,384]{0,1:T(8,128)(2,1)}, bf16[256,384]{0,1:T(8,128)(2,1)}, u32[]{:S(2)}, u32[]{:S(2)}) collective-permute-start(bf16[256,384]{0,1:T(8,128)(2,1)} %convert_element_type.149), channel_id=1, source_target_pairs={{0,1},{1,2},{2,3},{3,4},{4,5},{5,6},{6,7},{7,8},{8,9},{9,10},{10,1... | collective-permute-start | bytes 589832 | tf_op jit(solution)/shard_map/ppermute | solution.py:20
  76.5 1.4 collective-permute-start
  78.3 1.3 collective-permute-start.12
  80.8 8.6 %collective-permute-start.14 = (bf16[256,384]{0,1:T(8,128)(2,1)}, bf16[256,384]{0,1:T(8,128)(2,1)S(1)}, u32[]{:S(2)}, u32[]{:S(2)}) collective-permute-start(bf16[256,384]{0,1:T(8,128)(2,1)} %convert_element_type.149), channel_id=1, source_target_pairs={{0,4},{1,5},{2,6},{3,7},{4,8},{5,9},{6,10},{7,11},{8,12},{9,13},{1... | collective-permute-start | bytes 589832 | tf_op jit(solution)/shard_map/ppermute | solution.py:20
  89.7 1.5 fusion.105
  91.2 3.0 %collective-permute-done = bf16[256,384]{0,1:T(8,128)(2,1)S(1)} collective-permute-done((bf16[256,384]{0,1:T(8,128)(2,1)}, bf16[256,384]{0,1:T(8,128)(2,1)S(1)}, u32[]{:S(2)}, u32[]{:S(2)}) %collective-permute-start) | collective-permute-done | bytes 196640 | tf_op jit(solution)/shard_map/ppermute | solution.py:20
  101.3 9.1 %collective-permute-done.12 = bf16[256,384]{0,1:T(8,128)(2,1)S(1)} collective-permute-done((bf16[256,384]{0,1:T(8,128)(2,1)}, bf16[256,384]{0,1:T(8,128)(2,1)S(1)}, u32[]{:S(2)}, u32[]{:S(2)}) %collective-permute-start.12) | collective-permute-done | bytes 196640 | tf_op jit(solution)/shard_map/ppermute | solution.py:20
  114.1 81.9 %all-gather.3.cloned.1.call-done = f32[4096,768]{1,0:T(8,128)} async-done(((f32[256,768]{1,0:T(8,128)}), f32[4096,768]{1,0:T(8,128)}) %all-gather.3.cloned.1.call-update) | async-done | bytes 12582928 | tf_op jit(solution)/shard_map/all_gather | solution.py:14
  196.1 6.2 %reduce_sum.99 = bf16[256,768]{1,0:T(8,128)(2,1)} reduce(f32[16,256,768]{2,1,0:T(8,128)} %bitcast.258, f32[]{:T(128)} %constant.13.clone.1), dimensions={0}, to_apply=%region_1.2 | reduce | flops 2949120 | bytes 12976132 | tf_op jit(solution)/shard_map/reduce_sum | solution.py:14
  202.3 1.8 fusion.98
  204.1 1.7 copy.98
  205.8 2.7 %fusion.107 = (f32[256,3]{0,1:T(4,128)}, f32[256,3,256]{0,2,1:T(8,128)}) fusion(bf16[256,3,128]{0,2,1:T(8,128)(2,1)} %bitcast.285, bf16[256,3,128]{0,2,1:T(8,128)(2,1)S(1)} %convert_element_type.147), kind=kOutput, calls=%fused_computation.196 | convolution fusion | flops 50527488 | bytes 1182720 | tf_op jit(solution)/shard_map/qhd,khd->qhk/dot_general | solution.py:48
  208.5 1.8 copy.101
  211.1 1.4 fusion.37
  213.4 1.4 fusion.8
  214.8 1.5 fusion.11
  216.3 1.5 fusion.12
  217.8 1.5 fusion.13
  219.4 1.3 fusion.14
  220.7 1.3 fusion.15
  222.0 1.5 fusion.16
  (183 shorter events, 40.3 us)
Async XLA Ops:
  6.5 189.5 %all-gather.3.cloned.1.call-start = ((), (), s32[]{:S(2)}) async-start(), calls=%async_computation | async-start | bytes 13369344 | tf_op jit(solution)/shard_map/all_gather | solution.py:14
  14.7 61.7 %collective-permute-start.10 = (bf16[256,384]{0,1:T(8,128)(2,1)}, bf16[256,384]{0,1:T(8,128)(2,1)S(1)}, u32[]{:S(2)}, u32[]{:S(2)}) collective-permute-start(bf16[256,384]{0,1:T(8,128)(2,1)} %convert_element_type.149), channel_id=1, source_target_pairs={{0,3},{1,4},{2,5},{3,6},{4,7},{5,8},{6,9},{7,10},{8,11},{9,12},{10... | collective-permute-start | bytes 589832 | tf_op jit(solution)/shard_map/ppermute | solution.py:20
  20.6 16.9 %collective-permute-start.3 = (bf16[256,384]{1,0:T(8,128)(2,1)}, bf16[256,384]{1,0:T(8,128)(2,1)S(1)}, u32[]{:S(2)}, u32[]{:S(2)}) collective-permute-start(bf16[256,384]{1,0:T(8,128)(2,1)} %param.8), channel_id=1, source_target_pairs={{0,1},{1,2},{2,3},{3,4},{4,5},{5,6},{6,7},{7,8},{8,9},{9,10},{10,1... | collective-permute-start | bytes 589832 | tf_op jit(solution)/shard_map/ppermute | solution.py:20
  23.1 21.9 %collective-permute-start.5 = (bf16[256,384]{1,0:T(8,128)(2,1)}, bf16[256,384]{1,0:T(8,128)(2,1)S(1)}, u32[]{:S(2)}, u32[]{:S(2)}) collective-permute-start(bf16[256,384]{1,0:T(8,128)(2,1)} %param.8), channel_id=1, source_target_pairs={{2,0},{3,1},{4,2},{5,3},{6,4},{7,5},{8,6},{9,7},{10,8},{11,9},{12,... | collective-permute-start | bytes 589832 | tf_op jit(solution)/shard_map/ppermute | solution.py:20
  24.4 21.9 %collective-permute-start.7 = (bf16[256,384]{1,0:T(8,128)(2,1)}, bf16[256,384]{1,0:T(8,128)(2,1)S(1)}, u32[]{:S(2)}, u32[]{:S(2)}) collective-permute-start(bf16[256,384]{1,0:T(8,128)(2,1)} %param.8), channel_id=1, source_target_pairs={{0,2},{1,3},{2,4},{3,5},{4,6},{5,7},{6,8},{7,9},{8,10},{9,11},{10,... | collective-permute-start | bytes 589832 | tf_op jit(solution)/shard_map/ppermute | solution.py:20
  28.9 24.3 %collective-permute-start.9 = (bf16[256,384]{1,0:T(8,128)(2,1)}, bf16[256,384]{1,0:T(8,128)(2,1)S(1)}, u32[]{:S(2)}, u32[]{:S(2)}) collective-permute-start(bf16[256,384]{1,0:T(8,128)(2,1)} %param.8), channel_id=1, source_target_pairs={{3,0},{4,1},{5,2},{6,3},{7,4},{8,5},{9,6},{10,7},{11,8},{12,9},{13... | collective-permute-start | bytes 589832 | tf_op jit(solution)/shard_map/ppermute | solution.py:20
  31.3 22.0 %copy-start.27 = (f32[1,2,2,128]{3,1,2,0:T(2,128)}, f32[1,2,2,128]{3,1,2,0:T(2,128)S(1)}, u32[]{:S(2)}) copy-start(f32[1,2,2,128]{3,1,2,0:T(2,128)S(1)} %copy.200) | copy-start | bytes 6148
  33.8 19.5 %copy-start.29 = (f32[1,2,2,128]{3,1,2,0:T(2,128)}, f32[1,2,2,128]{3,1,2,0:T(2,128)S(1)}, u32[]{:S(2)}) copy-start(f32[1,2,2,128]{3,1,2,0:T(2,128)S(1)} %copy.201) | copy-start | bytes 6148
  35.0 18.3 %copy-start.37 = (f32[1,2,2,128]{3,1,2,0:T(2,128)}, f32[1,2,2,128]{3,1,2,0:T(2,128)S(1)}, u32[]{:S(2)}) copy-start(f32[1,2,2,128]{3,1,2,0:T(2,128)S(1)} %copy.204) | copy-start | bytes 6148
  35.2 18.1 %copy-start.38 = (f32[1,2,2,128]{3,1,2,0:T(2,128)}, f32[1,2,2,128]{3,1,2,0:T(2,128)S(1)}, u32[]{:S(2)}) copy-start(f32[1,2,2,128]{3,1,2,0:T(2,128)S(1)} %copy.205) | copy-start | bytes 6148
  36.0 17.3 %copy-start.31 = (f32[1,2,2,128]{3,1,2,0:T(2,128)}, f32[1,2,2,128]{3,1,2,0:T(2,128)S(1)}, u32[]{:S(2)}) copy-start(f32[1,2,2,128]{3,1,2,0:T(2,128)S(1)} %copy.199) | copy-start | bytes 6148
  36.8 16.5 %copy-start.34 = (f32[1,2,2,128]{3,1,2,0:T(2,128)}, f32[1,2,2,128]{3,1,2,0:T(2,128)S(1)}, u32[]{:S(2)}) copy-start(f32[1,2,2,128]{3,1,2,0:T(2,128)S(1)} %copy.198) | copy-start | bytes 6148
  37.5 20.7 %collective-permute-start.11 = (bf16[256,384]{1,0:T(8,128)(2,1)}, bf16[256,384]{1,0:T(8,128)(2,1)}, u32[]{:S(2)}, u32[]{:S(2)}) collective-permute-start(bf16[256,384]{1,0:T(8,128)(2,1)} %param.8), channel_id=1, source_target_pairs={{0,3},{1,4},{2,5},{3,6},{4,7},{5,8},{6,9},{7,10},{8,11},{9,12},{10... | collective-permute-start | bytes 589832 | tf_op jit(solution)/shard_map/ppermute | solution.py:20
  45.0 18.9 %collective-permute-start.13 = (bf16[256,384]{1,0:T(8,128)(2,1)}, bf16[256,384]{1,0:T(8,128)(2,1)S(1)}, u32[]{:S(2)}, u32[]{:S(2)}) collective-permute-start(bf16[256,384]{1,0:T(8,128)(2,1)} %param.8), channel_id=1, source_target_pairs={{4,0},{5,1},{6,2},{7,3},{8,4},{9,5},{10,6},{11,7},{12,8},{13,9},{1... | collective-permute-start | bytes 589832 | tf_op jit(solution)/shard_map/ppermute | solution.py:20
  46.2 22.0 %collective-permute-start.15 = (bf16[256,384]{1,0:T(8,128)(2,1)}, bf16[256,384]{1,0:T(8,128)(2,1)S(1)}, u32[]{:S(2)}, u32[]{:S(2)}) collective-permute-start(bf16[256,384]{1,0:T(8,128)(2,1)} %param.8), channel_id=1, source_target_pairs={{0,4},{1,5},{2,6},{3,7},{4,8},{5,9},{6,10},{7,11},{8,12},{9,13},{1... | collective-permute-start | bytes 589832 | tf_op jit(solution)/shard_map/ppermute | solution.py:20
  53.4 17.0 %collective-permute-start.1 = (bf16[256,384]{1,0:T(8,128)(2,1)}, bf16[256,384]{1,0:T(8,128)(2,1)S(1)}, u32[]{:S(2)}, u32[]{:S(2)}) collective-permute-start(bf16[256,384]{1,0:T(8,128)(2,1)} %param.8), channel_id=1, source_target_pairs={{1,0},{2,1},{3,2},{4,3},{5,4},{6,5},{7,6},{8,7},{9,8},{10,9},{11,1... | collective-permute-start | bytes 589832 | tf_op jit(solution)/shard_map/ppermute | solution.py:20
  58.2 20.0 %collective-permute-start.8 = (bf16[256,384]{0,1:T(8,128)(2,1)}, bf16[256,384]{0,1:T(8,128)(2,1)S(1)}, u32[]{:S(2)}, u32[]{:S(2)}) collective-permute-start(bf16[256,384]{0,1:T(8,128)(2,1)} %convert_element_type.149), channel_id=1, source_target_pairs={{3,0},{4,1},{5,2},{6,3},{7,4},{8,5},{9,6},{10,7},{11,8},{12,9},{13... | collective-permute-start | bytes 589832 | tf_op jit(solution)/shard_map/ppermute | solution.py:20
  63.8 17.0 %collective-permute-start.6 = (bf16[256,384]{0,1:T(8,128)(2,1)}, bf16[256,384]{0,1:T(8,128)(2,1)S(1)}, u32[]{:S(2)}, u32[]{:S(2)}) collective-permute-start(bf16[256,384]{0,1:T(8,128)(2,1)} %convert_element_type.149), channel_id=1, source_target_pairs={{0,2},{1,3},{2,4},{3,5},{4,6},{5,7},{6,8},{7,9},{8,10},{9,11},{10,... | collective-permute-start | bytes 589832 | tf_op jit(solution)/shard_map/ppermute | solution.py:20
  68.2 29.4 %collective-permute-start.4 = (bf16[256,384]{0,1:T(8,128)(2,1)}, bf16[256,384]{0,1:T(8,128)(2,1)}, u32[]{:S(2)}, u32[]{:S(2)}) collective-permute-start(bf16[256,384]{0,1:T(8,128)(2,1)} %convert_element_type.149), channel_id=1, source_target_pairs={{2,0},{3,1},{4,2},{5,3},{6,4},{7,5},{8,6},{9,7},{10,8},{11,9},{12,... | collective-permute-start | bytes 589832 | tf_op jit(solution)/shard_map/ppermute | solution.py:20
  70.4 19.4 %collective-permute-start.2 = (bf16[256,384]{0,1:T(8,128)(2,1)}, bf16[256,384]{0,1:T(8,128)(2,1)}, u32[]{:S(2)}, u32[]{:S(2)}) collective-permute-start(bf16[256,384]{0,1:T(8,128)(2,1)} %convert_element_type.149), channel_id=1, source_target_pairs={{0,1},{1,2},{2,3},{3,4},{4,5},{5,6},{6,7},{7,8},{8,9},{9,10},{10,1... | collective-permute-start | bytes 589832 | tf_op jit(solution)/shard_map/ppermute | solution.py:20
  76.4 33.9 %copy-start.19 = (pred[256,256]{0,1:T(8,128)(4,1)S(1)}, pred[256,256]{0,1:T(8,128)(4,1)}, u32[]{:S(2)}) copy-start(pred[256,256]{0,1:T(8,128)(4,1)} %bitcast_compare_fusion.1) | copy-start | bytes 196612
  76.4 34.3 %copy-start.30 = (f32[1,2,2,128]{3,1,2,0:T(2,128)S(1)}, f32[1,2,2,128]{3,1,2,0:T(2,128)}, u32[]{:S(2)}) copy-start(f32[1,2,2,128]{3,1,2,0:T(2,128)} %copy-done.29) | copy-start | bytes 6148
  76.4 34.3 %copy-start.28 = (f32[1,2,2,128]{3,1,2,0:T(2,128)S(1)}, f32[1,2,2,128]{3,1,2,0:T(2,128)}, u32[]{:S(2)}) copy-start(f32[1,2,2,128]{3,1,2,0:T(2,128)} %copy-done.27) | copy-start | bytes 6148
  76.4 35.4 %copy-start.18 = (pred[256,256]{0,1:T(8,128)(4,1)S(1)}, pred[256,256]{0,1:T(8,128)(4,1)}, u32[]{:S(2)}) copy-start(pred[256,256]{0,1:T(8,128)(4,1)} %bitcast_compare_fusion) | copy-start | bytes 196612
  76.4 35.8 %copy-start.32 = (f32[1,2,2,128]{3,1,2,0:T(2,128)S(1)}, f32[1,2,2,128]{3,1,2,0:T(2,128)}, u32[]{:S(2)}) copy-start(f32[1,2,2,128]{3,1,2,0:T(2,128)} %copy-done.31) | copy-start | bytes 6148
  76.4 35.8 %copy-start.35 = (f32[1,2,2,128]{3,1,2,0:T(2,128)S(1)}, f32[1,2,2,128]{3,1,2,0:T(2,128)}, u32[]{:S(2)}) copy-start(f32[1,2,2,128]{3,1,2,0:T(2,128)} %copy-done.34) | copy-start | bytes 6148
  76.5 17.8 %collective-permute-start = (bf16[256,384]{0,1:T(8,128)(2,1)}, bf16[256,384]{0,1:T(8,128)(2,1)S(1)}, u32[]{:S(2)}, u32[]{:S(2)}) collective-permute-start(bf16[256,384]{0,1:T(8,128)(2,1)} %convert_element_type.149), channel_id=1, source_target_pairs={{1,0},{2,1},{3,2},{4,3},{5,4},{6,5},{7,6},{8,7},{9,8},{10,9},{11,1... | collective-permute-start | bytes 589832 | tf_op jit(solution)/shard_map/ppermute | solution.py:20
  78.3 32.1 %collective-permute-start.12 = (bf16[256,384]{0,1:T(8,128)(2,1)}, bf16[256,384]{0,1:T(8,128)(2,1)S(1)}, u32[]{:S(2)}, u32[]{:S(2)}) collective-permute-start(bf16[256,384]{0,1:T(8,128)(2,1)} %convert_element_type.149), channel_id=1, source_target_pairs={{4,0},{5,1},{6,2},{7,3},{8,4},{9,5},{10,6},{11,7},{12,8},{13,9},{1... | collective-permute-start | bytes 589832 | tf_op jit(solution)/shard_map/ppermute | solution.py:20
  80.8 31.0 %collective-permute-start.14 = (bf16[256,384]{0,1:T(8,128)(2,1)}, bf16[256,384]{0,1:T(8,128)(2,1)S(1)}, u32[]{:S(2)}, u32[]{:S(2)}) collective-permute-start(bf16[256,384]{0,1:T(8,128)(2,1)} %convert_element_type.149), channel_id=1, source_target_pairs={{0,4},{1,5},{2,6},{3,7},{4,8},{5,9},{6,10},{7,11},{8,12},{9,13},{1... | collective-permute-start | bytes 589832 | tf_op jit(solution)/shard_map/ppermute | solution.py:20
  89.7 22.5 %copy-start.21 = (f32[256,3]{0,1:T(4,128)}, f32[256,3]{0,1:T(4,128)S(1)}, u32[]{:S(2)}) copy-start(f32[256,3]{0,1:T(4,128)S(1)} %get-tuple-element.57) | copy-start | bytes 9220
  208.5 15.6 %copy-start.16 = (bf16[256,384]{0,1:T(8,128)(2,1)S(1)}, bf16[256,384]{0,1:T(8,128)(2,1)}, u32[]{:S(2)}) copy-start(bf16[256,384]{0,1:T(8,128)(2,1)} %copy.106) | copy-start | bytes 589828
  210.3 13.8 %copy-start.7 = (f32[256,2,128]{0,2,1:T(8,128)S(1)}, f32[256,2,128]{0,2,1:T(8,128)}, u32[]{:S(2)}) copy-start(f32[256,2,128]{0,2,1:T(8,128)} %copy-done.6) | copy-start | bytes 786436
  (24 other events, 145.9 us)
Sparse Core Ops, SparseCore 0:
  14.8 181.1 all-gather.2
